TPU v7x, 512 devices: a whole 4x8x8 slice. The times are simulated.
512 devices in a mesh: ctx: 16 (over z_hi, y), dp: 32 (over z_lo, x, core).
Axes of the slice: x: 4, y: 8, z: 8 (z_hi: 2, z_lo: 4; z = z_hi * 4 + z_lo), core: 2. Of those that a mesh axis runs over, the one named last changes fastest.
Arguments:
- queries: bfloat16 [32, 2048, 2048], P('dp', 'ctx'), may hold values from -8 to 8
- key_rows: bfloat16 [32, 2048, 256], P('dp', 'ctx'), may hold values from -8 to 8
- value_rows: bfloat16 [32, 2048, 256], P('dp', 'ctx'), may hold values from -6 to 6
- stream: bfloat16 [32, 2048, 2048], P('dp', 'ctx'), may hold values from -6 to 6
- norm_gain: float32 [2048], replicated, may hold values from 0.1 to 1.9
- expert_ids: int32 [32, 2048, 8], P('dp', 'ctx'), may hold values from 0 to 127, all different within a row; in each aligned block of 128 rows (0 to 127, 128 to 255, ..., all dimensions but the last counted through in order) at most 12 rows name the same one
- gate_values: float32 [32, 2048, 8], P('dp', 'ctx'), may hold values from 0.1 to 1
- w_gate: bfloat16 [32, 2048, 384], P('dp', 'ctx'), may hold values from -0.125 to 0.125
- w_up: bfloat16 [32, 2048, 384], P('dp', 'ctx'), may hold values from -0.125 to 0.125
- w_down: bfloat16 [32, 384, 2048], P('dp', None, 'ctx'), may hold values from -0.3125 to 0.3125
Outputs:
- attended: bfloat16 [32, 2048, 2048], P('dp', 'ctx')
- expert_out: bfloat16 [32, 2048, 2048], P('dp', 'ctx')
Inputs may be any that keep to these rules, and one draw needn't show every extreme that they name: `expert_ids`: among the rows of one device, no expert is chosen by more than 12 rows; some expert reaches 12.
All inputs are finite; a program needn't handle non-finite values.
Results may differ from a plain program's by a relative error of at most 0.012.
Values may be sent and summed in bfloat16 or wider, within the bound.
No kernel may reach another device: no remote copies, remote signals or barrier semaphores. Data moves between devices by JAX's collectives and lax.ppermute only.
A program may use at most 64 MiB of HBM per device.

v0:
```python
import math
import jax
import jax.numpy as jnp
from jax import lax
from jax.sharding import PartitionSpec as P

HD = 128
CAP = 12
masked_score = -1e30


def passed_along(block, axis, distance):
    devices = range(lax.axis_size(axis))
    route = [(i - distance, i) for i in devices if i - distance in devices]
    return lax.ppermute(block, axis, route)


def attend_block(state, query_blocks, key_block, value_block, query_pos, key_start):
    largest, total, accum = state
    scale = 1.0 / math.sqrt(query_blocks.shape[-1])
    scores = (
        jnp.einsum("hrd,hkd->hrk", query_blocks, key_block, preferred_element_type=jnp.float32)
        * scale
    )
    key_pos = key_start + jnp.arange(key_block.shape[1], dtype=jnp.int32)
    allowed = key_pos[None, None, :] <= query_pos[None, :, None]
    block_max = jnp.max(jnp.where(allowed, scores, masked_score), axis=-1)
    new_max = jnp.maximum(largest, block_max)
    weights = jnp.where(allowed, jnp.exp(scores - new_max[..., None]), 0.0)
    rescale = jnp.exp(largest - new_max)
    total = total * rescale + jnp.sum(weights, axis=-1)
    accum = accum * rescale[..., None] + jnp.einsum(
        "hrk,hkd->hrd",
        weights.astype(jnp.bfloat16),
        value_block,
        preferred_element_type=jnp.float32,
    )
    return (new_max, total, accum)


def shards(
    queries, key_rows, value_rows, stream, norm_gain, expert_ids, gate_values, w_gate, w_up, w_down
):
    tokens = queries.shape[1]
    heads_kv = key_rows.shape[2] // HD
    group = queries.shape[2] // key_rows.shape[2]
    query_blocks = (
        queries[0]
        .reshape(tokens, heads_kv, group, HD)
        .transpose(1, 2, 0, 3)
        .reshape(heads_kv, group * tokens, HD)
    )
    key_local = key_rows[0].reshape(tokens, heads_kv, HD).transpose(1, 0, 2)
    value_local = value_rows[0].reshape(tokens, heads_kv, HD).transpose(1, 0, 2)
    block_pos = lax.axis_index("ctx")
    block_count = lax.axis_size("ctx")
    query_pos = block_pos * tokens + jnp.arange(group * tokens, dtype=jnp.int32) % tokens
    last_query = block_pos * tokens + tokens - 1
    state = (
        jnp.full((heads_kv, group * tokens), masked_score, jnp.float32),
        jnp.zeros((heads_kv, group * tokens), jnp.float32),
        jnp.zeros((heads_kv, group * tokens, HD), jnp.float32),
    )

    def maybe_attend(current, key_block, value_block, key_start):

        def compute(inner):
            return attend_block(inner, query_blocks, key_block, value_block, query_pos, key_start)

        def unchanged(inner):
            return inner

        return lax.cond(key_start <= last_query, compute, unchanged, current)

    state = attend_block(state, query_blocks, key_local, value_local, query_pos, block_pos * tokens)

    def pass_turn(turn, carry):
        current, key_block, value_block = carry
        key_block, value_block = passed_along((key_block, value_block), "ctx", 1)
        source = (block_pos - turn - 1) % block_count
        current = maybe_attend(current, key_block, value_block, source * tokens)
        return (current, key_block, value_block)

    state, key_last, value_last = lax.fori_loop(
        0, block_count - 1, pass_turn, (state, key_local, value_local)
    )
    largest, total, accum = state
    attended = (accum / total[..., None]).reshape(heads_kv, group, tokens, HD).transpose(2, 0, 1, 3)
    attended = attended.reshape(1, tokens, heads_kv * group * HD).astype(jnp.bfloat16)
    width = stream.shape[2]
    rows_in = stream[0].astype(jnp.float32)
    normed = (
        rows_in * lax.rsqrt(jnp.mean(rows_in * rows_in, axis=-1, keepdims=True) + 1e-06) * norm_gain
    ).astype(jnp.bfloat16)
    owners = lax.axis_size("dp")
    slots = owners * CAP
    top_count = expert_ids.shape[2]
    chosen = expert_ids[0].reshape(-1)
    weights_flat = gate_values[0].reshape(-1)
    owner_hot = (chosen[:, None] == jnp.arange(owners, dtype=jnp.int32)[None, :]).astype(jnp.int32)
    ranks = jnp.sum((jnp.cumsum(owner_hot, axis=0) - 1) * owner_hot, axis=1)
    target = jnp.where(chosen < owners, chosen * CAP + ranks, -1)
    slot_hot = target[:, None] == jnp.arange(slots, dtype=jnp.int32)[None, :]
    placement = jnp.sum(
        slot_hot.astype(jnp.float32).reshape(tokens, top_count, slots), axis=1
    ).astype(jnp.bfloat16)
    slot_weight = jnp.sum(jnp.where(slot_hot, weights_flat[:, None], 0.0), axis=0)
    outgoing = jnp.einsum(
        "ts,td->sd", placement, normed, preferred_element_type=jnp.float32
    ).astype(jnp.bfloat16)
    arrived = lax.all_to_all(
        outgoing.reshape(owners, CAP, width), "dp", split_axis=0, concat_axis=0, tiled=True
    ).reshape(slots, width)
    gate_piece = lax.all_gather(w_gate, "ctx", axis=1, tiled=True)
    up_piece = lax.all_gather(w_up, "ctx", axis=1, tiled=True)
    gate_sum = jnp.dot(arrived, gate_piece[0], preferred_element_type=jnp.float32)
    up_sum = jnp.dot(arrived, up_piece[0], preferred_element_type=jnp.float32)
    hidden = (jax.nn.silu(gate_sum) * up_sum).astype(jnp.bfloat16)
    produced = jnp.dot(
        hidden,
        lax.all_gather(w_down, "ctx", axis=2, tiled=True)[0],
        preferred_element_type=jnp.float32,
    )
    answers = produced.astype(jnp.bfloat16).reshape(owners, CAP, width)
    returned = lax.all_to_all(answers, "dp", split_axis=0, concat_axis=0, tiled=True).reshape(
        slots, width
    )
    weighted = returned.astype(jnp.float32) * slot_weight[:, None]
    upper_part = weighted.astype(jnp.bfloat16)
    lower_part = (weighted - upper_part.astype(jnp.float32)).astype(jnp.bfloat16)
    mixed = jnp.dot(placement, upper_part, preferred_element_type=jnp.float32) + jnp.dot(
        placement, lower_part, preferred_element_type=jnp.float32
    )
    expert_out = mixed.astype(jnp.bfloat16).reshape(1, tokens, width)
    return (attended, expert_out)


def solution(mesh):
    placed = (
        P("dp", "ctx", None),
        P("dp", "ctx", None),
        P("dp", "ctx", None),
        P("dp", "ctx", None),
        P(),
        P("dp", "ctx", None),
        P("dp", "ctx", None),
        P("dp", "ctx", None),
        P("dp", "ctx", None),
        P("dp", None, "ctx"),
    )
    return jax.shard_map(
        shards,
        mesh=mesh,
        in_specs=placed,
        out_specs=(P("dp", "ctx", None), P("dp", "ctx", None)),
        check_vma=False,
    )
```

profile of v0, /device:TPU:62, one launch (start us, length us, event | category | flops | bytes accessed | tf_op | source)
XLA Modules:
  0.0 572.4 jit_solution(15209295898949841804)
XLA Ops:
  9.7 9.0 %reduce-window.6 = s32[32,8,128]{2,1,0:T(8,128)S(1)} reduce-window(s32[32,8,128]{2,1,0:T(8,128)S(1)} %fusion.49, s32[]{:T(128)} %constant.106.clone.1), window={size=1x1x128 pad=0_0x0_0x127_0}, to_apply=%region_8.9 | reduce-window | flops 4161536 | bytes 262148 | tf_op jit(solution)/shard_map/reduce-window
  22.2 10.5 %all-to-all-start = ((bf16[32,12,2048]{2,1,0:T(8,128)(2,1)}), bf16[32,12,2048]{2,1,0:T(8,128)(2,1)}, u32[]{:S(2)}, u32[]{:S(2)}) async-start(bf16[32,12,2048]{2,1,0:T(8,128)(2,1)} %reshape.192), calls=%async_computation | async-start | bytes 4194304 | tf_op jit(solution)/shard_map/all_to_all | solution.py:111
  35.1 64.5 %all-to-all-done = bf16[32,12,2048]{2,1,0:T(8,128)(2,1)} async-done(((bf16[32,12,2048]{2,1,0:T(8,128)(2,1)}), bf16[32,12,2048]{2,1,0:T(8,128)(2,1)}, u32[]{:S(2)}, u32[]{:S(2)}) %all-to-all-start) | async-done | bytes 1572896 | tf_op jit(solution)/shard_map/all_to_all | solution.py:111
  99.6 3.6 reshape.193
  103.2 3.9 all-gather.4.cloned.1.call-done
  107.1 2.8 fusion.16
  110.0 103.4 %all-gather.6.cloned.1.call-done = bf16[1,2048,384]{2,1,0:T(8,128)(2,1)} async-done(((bf16[1,128,384]{2,1,0:T(8,128)(2,1)}), bf16[1,2048,384]{2,1,0:T(8,128)(2,1)}) %all-gather.6.cloned.1.call-update) | async-done | bytes 1572880 | tf_op jit(solution)/shard_map/all_gather | solution.py:115
  213.4 97.3 %all-gather.8.cloned.1.call-done = bf16[1,384,2048]{2,1,0:T(8,128)(2,1)} async-done(((bf16[1,384,128]{2,1,0:T(8,128)(2,1)}), bf16[1,384,2048]{2,1,0:T(8,128)(2,1)}) %all-gather.8.cloned.1.call-update) | async-done | bytes 1572880 | tf_op jit(solution)/shard_map/all_gather | solution.py:121
  310.6 5.4 convolution_convert_fusion
  316.0 3.6 reshape.194
  319.6 5.4 all-to-all-start.1
  326.1 233.3 %while.24 = (s32[]{:T(128)}, f32[2,1024]{1,0:T(2,128)S(1)}, f32[2,1024]{1,0:T(2,128)S(1)}, f32[2,1024,128]{2,1,0:T(8,128)S(1)}, bf16[2,128,128]{2,1,0:T(8,128)(2...) while((s32[]{:T(128)}, f32[2,1024]{1,0:T(2,128)S(1)}, ...), condition=%wide.region_7.8_spmd.clone, body=%wide.region_2.7_spmd.clone.sunk | while | flops 137243792 | bytes 7378492 | solution.py:84
  326.1 4.6 collective-permute-start
  330.8 2.5 collective-permute-start.1
  333.3 3.6 collective-permute-done.1
  336.9 1.6 conditional.3
  338.6 10.2 %collective-permute-start = (bf16[2,128,128]{2,1,0:T(8,128)(2,1)S(1)}, bf16[2,128,128]{2,1,0:T(8,128)(2,1)S(1)}, u32[]{:S(2)}, u32[]{:S(2)}) collective-permute-start(bf16[2,128,128]{2,1,0:T(8,128)(2,1)S(1)} %get-tuple-element.508), channel_id=1, source_target_pairs={{0,32},{32,64},{64,96},{96,128},{128,160},{160,192},{192,224},{224... | collective-permute-start | bytes 196616 | tf_op jit(solution)/shard_map/while/body/eval_jaxpr/ppermute | solution.py:15
  348.8 1.9 collective-permute-start.1
  350.8 4.2 collective-permute-done.1
  355.0 1.6 conditional.3
  356.7 8.7 %collective-permute-start = (bf16[2,128,128]{2,1,0:T(8,128)(2,1)S(1)}, bf16[2,128,128]{2,1,0:T(8,128)(2,1)S(1)}, u32[]{:S(2)}, u32[]{:S(2)}) collective-permute-start(bf16[2,128,128]{2,1,0:T(8,128)(2,1)S(1)} %get-tuple-element.508), channel_id=1, source_target_pairs={{0,32},{32,64},{64,96},{96,128},{128,160},{160,192},{192,224},{224... | collective-permute-start | bytes 196616 | tf_op jit(solution)/shard_map/while/body/eval_jaxpr/ppermute | solution.py:15
  365.4 1.9 collective-permute-start.1
  367.4 4.2 collective-permute-done.1
  371.6 1.6 conditional.3
  373.3 8.7 %collective-permute-start = (bf16[2,128,128]{2,1,0:T(8,128)(2,1)S(1)}, bf16[2,128,128]{2,1,0:T(8,128)(2,1)S(1)}, u32[]{:S(2)}, u32[]{:S(2)}) collective-permute-start(bf16[2,128,128]{2,1,0:T(8,128)(2,1)S(1)} %get-tuple-element.508), channel_id=1, source_target_pairs={{0,32},{32,64},{64,96},{96,128},{128,160},{160,192},{192,224},{224... | collective-permute-start | bytes 196616 | tf_op jit(solution)/shard_map/while/body/eval_jaxpr/ppermute | solution.py:15
  382.0 1.9 collective-permute-start.1
  384.0 4.2 collective-permute-done.1
  388.2 1.6 conditional.3
  389.9 8.2 %collective-permute-start = (bf16[2,128,128]{2,1,0:T(8,128)(2,1)S(1)}, bf16[2,128,128]{2,1,0:T(8,128)(2,1)S(1)}, u32[]{:S(2)}, u32[]{:S(2)}) collective-permute-start(bf16[2,128,128]{2,1,0:T(8,128)(2,1)S(1)} %get-tuple-element.508), channel_id=1, source_target_pairs={{0,32},{32,64},{64,96},{96,128},{128,160},{160,192},{192,224},{224... | collective-permute-start | bytes 196616 | tf_op jit(solution)/shard_map/while/body/eval_jaxpr/ppermute | solution.py:15
  398.1 1.9 collective-permute-start.1
  400.0 4.2 collective-permute-done.1
  404.2 1.6 conditional.3
  405.9 8.2 %collective-permute-start = (bf16[2,128,128]{2,1,0:T(8,128)(2,1)S(1)}, bf16[2,128,128]{2,1,0:T(8,128)(2,1)S(1)}, u32[]{:S(2)}, u32[]{:S(2)}) collective-permute-start(bf16[2,128,128]{2,1,0:T(8,128)(2,1)S(1)} %get-tuple-element.508), channel_id=1, source_target_pairs={{0,32},{32,64},{64,96},{96,128},{128,160},{160,192},{192,224},{224... | collective-permute-start | bytes 196616 | tf_op jit(solution)/shard_map/while/body/eval_jaxpr/ppermute | solution.py:15
  414.1 1.9 collective-permute-start.1
  416.1 4.8 collective-permute-done.1
  422.6 7.6 %collective-permute-start = (bf16[2,128,128]{2,1,0:T(8,128)(2,1)S(1)}, bf16[2,128,128]{2,1,0:T(8,128)(2,1)S(1)}, u32[]{:S(2)}, u32[]{:S(2)}) collective-permute-start(bf16[2,128,128]{2,1,0:T(8,128)(2,1)S(1)} %get-tuple-element.508), channel_id=1, source_target_pairs={{0,32},{32,64},{64,96},{96,128},{128,160},{160,192},{192,224},{224... | collective-permute-start | bytes 196616 | tf_op jit(solution)/shard_map/while/body/eval_jaxpr/ppermute | solution.py:15
  430.2 1.9 collective-permute-start.1
  432.2 4.5 collective-permute-done.1
  436.6 1.6 conditional.3
  438.3 7.9 %collective-permute-start = (bf16[2,128,128]{2,1,0:T(8,128)(2,1)S(1)}, bf16[2,128,128]{2,1,0:T(8,128)(2,1)S(1)}, u32[]{:S(2)}, u32[]{:S(2)}) collective-permute-start(bf16[2,128,128]{2,1,0:T(8,128)(2,1)S(1)} %get-tuple-element.508), channel_id=1, source_target_pairs={{0,32},{32,64},{64,96},{96,128},{128,160},{160,192},{192,224},{224... | collective-permute-start | bytes 196616 | tf_op jit(solution)/shard_map/while/body/eval_jaxpr/ppermute | solution.py:15
  446.3 1.9 collective-permute-start.1
  448.2 4.2 collective-permute-done.1
  452.5 9.8 %collective-permute-start = (bf16[2,128,128]{2,1,0:T(8,128)(2,1)S(1)}, bf16[2,128,128]{2,1,0:T(8,128)(2,1)S(1)}, u32[]{:S(2)}, u32[]{:S(2)}) collective-permute-start(bf16[2,128,128]{2,1,0:T(8,128)(2,1)S(1)} %get-tuple-element.508), channel_id=1, source_target_pairs={{0,32},{32,64},{64,96},{96,128},{128,160},{160,192},{192,224},{224... | collective-permute-start | bytes 196616 | tf_op jit(solution)/shard_map/while/body/eval_jaxpr/ppermute | solution.py:15
  462.3 1.9 collective-permute-start.1
  464.3 4.2 collective-permute-done.1
  468.5 8.2 %collective-permute-start = (bf16[2,128,128]{2,1,0:T(8,128)(2,1)S(1)}, bf16[2,128,128]{2,1,0:T(8,128)(2,1)S(1)}, u32[]{:S(2)}, u32[]{:S(2)}) collective-permute-start(bf16[2,128,128]{2,1,0:T(8,128)(2,1)S(1)} %get-tuple-element.508), channel_id=1, source_target_pairs={{0,32},{32,64},{64,96},{96,128},{128,160},{160,192},{192,224},{224... | collective-permute-start | bytes 196616 | tf_op jit(solution)/shard_map/while/body/eval_jaxpr/ppermute | solution.py:15
  476.7 1.9 collective-permute-start.1
  478.7 4.2 collective-permute-done.1
  482.9 9.1 %collective-permute-start = (bf16[2,128,128]{2,1,0:T(8,128)(2,1)S(1)}, bf16[2,128,128]{2,1,0:T(8,128)(2,1)S(1)}, u32[]{:S(2)}, u32[]{:S(2)}) collective-permute-start(bf16[2,128,128]{2,1,0:T(8,128)(2,1)S(1)} %get-tuple-element.508), channel_id=1, source_target_pairs={{0,32},{32,64},{64,96},{96,128},{128,160},{160,192},{192,224},{224... | collective-permute-start | bytes 196616 | tf_op jit(solution)/shard_map/while/body/eval_jaxpr/ppermute | solution.py:15
  492.0 1.9 collective-permute-start.1
  494.0 4.4 collective-permute-done.1
  498.4 9.0 %collective-permute-start = (bf16[2,128,128]{2,1,0:T(8,128)(2,1)S(1)}, bf16[2,128,128]{2,1,0:T(8,128)(2,1)S(1)}, u32[]{:S(2)}, u32[]{:S(2)}) collective-permute-start(bf16[2,128,128]{2,1,0:T(8,128)(2,1)S(1)} %get-tuple-element.508), channel_id=1, source_target_pairs={{0,32},{32,64},{64,96},{96,128},{128,160},{160,192},{192,224},{224... | collective-permute-start | bytes 196616 | tf_op jit(solution)/shard_map/while/body/eval_jaxpr/ppermute | solution.py:15
  507.4 1.9 collective-permute-start.1
  509.7 4.1 collective-permute-done.1
  513.9 9.5 %collective-permute-start = (bf16[2,128,128]{2,1,0:T(8,128)(2,1)S(1)}, bf16[2,128,128]{2,1,0:T(8,128)(2,1)S(1)}, u32[]{:S(2)}, u32[]{:S(2)}) collective-permute-start(bf16[2,128,128]{2,1,0:T(8,128)(2,1)S(1)} %get-tuple-element.508), channel_id=1, source_target_pairs={{0,32},{32,64},{64,96},{96,128},{128,160},{160,192},{192,224},{224... | collective-permute-start | bytes 196616 | tf_op jit(solution)/shard_map/while/body/eval_jaxpr/ppermute | solution.py:15
  523.5 1.9 collective-permute-start.1
  525.4 4.2 collective-permute-done.1
  529.7 8.8 %collective-permute-start = (bf16[2,128,128]{2,1,0:T(8,128)(2,1)S(1)}, bf16[2,128,128]{2,1,0:T(8,128)(2,1)S(1)}, u32[]{:S(2)}, u32[]{:S(2)}) collective-permute-start(bf16[2,128,128]{2,1,0:T(8,128)(2,1)S(1)} %get-tuple-element.508), channel_id=1, source_target_pairs={{0,32},{32,64},{64,96},{96,128},{128,160},{160,192},{192,224},{224... | collective-permute-start | bytes 196616 | tf_op jit(solution)/shard_map/while/body/eval_jaxpr/ppermute | solution.py:15
  538.5 1.9 collective-permute-start.1
  540.9 3.8 collective-permute-done.1
  544.7 8.5 %collective-permute-start = (bf16[2,128,128]{2,1,0:T(8,128)(2,1)S(1)}, bf16[2,128,128]{2,1,0:T(8,128)(2,1)S(1)}, u32[]{:S(2)}, u32[]{:S(2)}) collective-permute-start(bf16[2,128,128]{2,1,0:T(8,128)(2,1)S(1)} %get-tuple-element.508), channel_id=1, source_target_pairs={{0,32},{32,64},{64,96},{96,128},{128,160},{160,192},{192,224},{224... | collective-permute-start | bytes 196616 | tf_op jit(solution)/shard_map/while/body/eval_jaxpr/ppermute | solution.py:15
  553.2 1.9 collective-permute-start.1
  555.2 4.2 collective-permute-done.1
  561.5 2.5 reshape.197
  (207 shorter events, 27.0 us)
Async XLA Ops:
  7.2 12.7 %copy-start = (bf16[1,128,2048]{2,1,0:T(8,128)(2,1)S(1)}, bf16[1,128,2048]{2,1,0:T(8,128)(2,1)}, u32[]{:S(2)}) copy-start(bf16[1,128,2048]{2,1,0:T(8,128)(2,1)} %param.17) | copy-start | bytes 1572868
  7.2 12.9 %copy-start.4 = (f32[2048]{0:T(1024)S(1)}, f32[2048]{0:T(1024)}, u32[]{:S(2)}) copy-start(f32[2048]{0:T(1024)} %param.18) | copy-start | bytes 24580
  7.2 99.9 %all-gather.4.cloned.1.call-start = ((), (), s32[]{:S(2)}) async-start(), calls=%async_computation.2 | async-start | bytes 1671168 | tf_op jit(solution)/shard_map/all_gather | solution.py:114
  7.9 205.5 %all-gather.6.cloned.1.call-start = ((), (), s32[]{:S(2)}) async-start(), calls=%async_computation.3 | async-start | bytes 1671168 | tf_op jit(solution)/shard_map/all_gather | solution.py:115
  22.2 11.3 %copy-start.5 = (f32[1,128,8]{1,2,0:T(8,128)S(1)}, f32[1,128,8]{1,2,0:T(8,128)}, u32[]{:S(2)}) copy-start(f32[1,128,8]{1,2,0:T(8,128)} %param.20) | copy-start | bytes 12292
  22.2 11.5 %copy-start.1 = (bf16[1,128,2048]{2,1,0:T(8,128)(2,1)S(1)}, bf16[1,128,2048]{2,1,0:T(8,128)(2,1)}, u32[]{:S(2)}) copy-start(bf16[1,128,2048]{2,1,0:T(8,128)(2,1)} %param.14) | copy-start | bytes 1572868
  22.2 77.4 %all-to-all-start = ((bf16[32,12,2048]{2,1,0:T(8,128)(2,1)}), bf16[32,12,2048]{2,1,0:T(8,128)(2,1)}, u32[]{:S(2)}, u32[]{:S(2)}) async-start(bf16[32,12,2048]{2,1,0:T(8,128)(2,1)} %reshape.192), calls=%async_computation | async-start | bytes 4194304 | tf_op jit(solution)/shard_map/all_to_all | solution.py:111
  32.8 1.2 copy-start.2
  32.8 1.4 copy-start.3
  32.8 277.9 %all-gather.8.cloned.1.call-start = ((), (), s32[]{:S(2)}) async-start(), calls=%async_computation.4 | async-start | bytes 1671168 | tf_op jit(solution)/shard_map/all_gather | solution.py:121
  319.6 241.9 %all-to-all-start.1 = ((bf16[32,12,2048]{2,1,0:T(8,128)(2,1)}), bf16[32,12,2048]{2,1,0:T(8,128)(2,1)}, u32[]{:S(2)}, u32[]{:S(2)}) async-start(bf16[32,12,2048]{2,1,0:T(8,128)(2,1)} %reshape.194), calls=%async_computation.1 | async-start | bytes 4194304 | tf_op jit(solution)/shard_map/all_to_all | solution.py:125
  326.1 7.2 %collective-permute-start = (bf16[2,128,128]{2,1,0:T(8,128)(2,1)S(1)}, bf16[2,128,128]{2,1,0:T(8,128)(2,1)S(1)}, u32[]{:S(2)}, u32[]{:S(2)}) collective-permute-start(bf16[2,128,128]{2,1,0:T(8,128)(2,1)S(1)} %get-tuple-element.508), channel_id=1, source_target_pairs={{0,32},{32,64},{64,96},{96,128},{128,160},{160,192},{192,224},{224... | collective-permute-start | bytes 196616 | tf_op jit(solution)/shard_map/while/body/eval_jaxpr/ppermute | solution.py:15
  330.8 6.2 %collective-permute-start.1 = (bf16[2,128,128]{2,1,0:T(8,128)(2,1)S(1)}, bf16[2,128,128]{2,1,0:T(8,128)(2,1)S(1)}, u32[]{:S(2)}, u32[]{:S(2)}) collective-permute-start(bf16[2,128,128]{2,1,0:T(8,128)(2,1)S(1)} %get-tuple-element.509), channel_id=1, source_target_pairs={{0,32},{32,64},{64,96},{96,128},{128,160},{160,192},{192,224},{224... | collective-permute-start | bytes 196616 | tf_op jit(solution)/shard_map/while/body/eval_jaxpr/ppermute | solution.py:15
  338.6 12.2 %collective-permute-start = (bf16[2,128,128]{2,1,0:T(8,128)(2,1)S(1)}, bf16[2,128,128]{2,1,0:T(8,128)(2,1)S(1)}, u32[]{:S(2)}, u32[]{:S(2)}) collective-permute-start(bf16[2,128,128]{2,1,0:T(8,128)(2,1)S(1)} %get-tuple-element.508), channel_id=1, source_target_pairs={{0,32},{32,64},{64,96},{96,128},{128,160},{160,192},{192,224},{224... | collective-permute-start | bytes 196616 | tf_op jit(solution)/shard_map/while/body/eval_jaxpr/ppermute | solution.py:15
  348.8 6.2 %collective-permute-start.1 = (bf16[2,128,128]{2,1,0:T(8,128)(2,1)S(1)}, bf16[2,128,128]{2,1,0:T(8,128)(2,1)S(1)}, u32[]{:S(2)}, u32[]{:S(2)}) collective-permute-start(bf16[2,128,128]{2,1,0:T(8,128)(2,1)S(1)} %get-tuple-element.509), channel_id=1, source_target_pairs={{0,32},{32,64},{64,96},{96,128},{128,160},{160,192},{192,224},{224... | collective-permute-start | bytes 196616 | tf_op jit(solution)/shard_map/while/body/eval_jaxpr/ppermute | solution.py:15
  356.7 10.7 %collective-permute-start = (bf16[2,128,128]{2,1,0:T(8,128)(2,1)S(1)}, bf16[2,128,128]{2,1,0:T(8,128)(2,1)S(1)}, u32[]{:S(2)}, u32[]{:S(2)}) collective-permute-start(bf16[2,128,128]{2,1,0:T(8,128)(2,1)S(1)} %get-tuple-element.508), channel_id=1, source_target_pairs={{0,32},{32,64},{64,96},{96,128},{128,160},{160,192},{192,224},{224... | collective-permute-start | bytes 196616 | tf_op jit(solution)/shard_map/while/body/eval_jaxpr/ppermute | solution.py:15
  365.4 6.2 %collective-permute-start.1 = (bf16[2,128,128]{2,1,0:T(8,128)(2,1)S(1)}, bf16[2,128,128]{2,1,0:T(8,128)(2,1)S(1)}, u32[]{:S(2)}, u32[]{:S(2)}) collective-permute-start(bf16[2,128,128]{2,1,0:T(8,128)(2,1)S(1)} %get-tuple-element.509), channel_id=1, source_target_pairs={{0,32},{32,64},{64,96},{96,128},{128,160},{160,192},{192,224},{224... | collective-permute-start | bytes 196616 | tf_op jit(solution)/shard_map/while/body/eval_jaxpr/ppermute | solution.py:15
  373.3 10.7 %collective-permute-start = (bf16[2,128,128]{2,1,0:T(8,128)(2,1)S(1)}, bf16[2,128,128]{2,1,0:T(8,128)(2,1)S(1)}, u32[]{:S(2)}, u32[]{:S(2)}) collective-permute-start(bf16[2,128,128]{2,1,0:T(8,128)(2,1)S(1)} %get-tuple-element.508), channel_id=1, source_target_pairs={{0,32},{32,64},{64,96},{96,128},{128,160},{160,192},{192,224},{224... | collective-permute-start | bytes 196616 | tf_op jit(solution)/shard_map/while/body/eval_jaxpr/ppermute | solution.py:15
  382.0 6.2 %collective-permute-start.1 = (bf16[2,128,128]{2,1,0:T(8,128)(2,1)S(1)}, bf16[2,128,128]{2,1,0:T(8,128)(2,1)S(1)}, u32[]{:S(2)}, u32[]{:S(2)}) collective-permute-start(bf16[2,128,128]{2,1,0:T(8,128)(2,1)S(1)} %get-tuple-element.509), channel_id=1, source_target_pairs={{0,32},{32,64},{64,96},{96,128},{128,160},{160,192},{192,224},{224... | collective-permute-start | bytes 196616 | tf_op jit(solution)/shard_map/while/body/eval_jaxpr/ppermute | solution.py:15
  389.9 10.2 %collective-permute-start = (bf16[2,128,128]{2,1,0:T(8,128)(2,1)S(1)}, bf16[2,128,128]{2,1,0:T(8,128)(2,1)S(1)}, u32[]{:S(2)}, u32[]{:S(2)}) collective-permute-start(bf16[2,128,128]{2,1,0:T(8,128)(2,1)S(1)} %get-tuple-element.508), channel_id=1, source_target_pairs={{0,32},{32,64},{64,96},{96,128},{128,160},{160,192},{192,224},{224... | collective-permute-start | bytes 196616 | tf_op jit(solution)/shard_map/while/body/eval_jaxpr/ppermute | solution.py:15
  398.1 6.2 %collective-permute-start.1 = (bf16[2,128,128]{2,1,0:T(8,128)(2,1)S(1)}, bf16[2,128,128]{2,1,0:T(8,128)(2,1)S(1)}, u32[]{:S(2)}, u32[]{:S(2)}) collective-permute-start(bf16[2,128,128]{2,1,0:T(8,128)(2,1)S(1)} %get-tuple-element.509), channel_id=1, source_target_pairs={{0,32},{32,64},{64,96},{96,128},{128,160},{160,192},{192,224},{224... | collective-permute-start | bytes 196616 | tf_op jit(solution)/shard_map/while/body/eval_jaxpr/ppermute | solution.py:15
  405.9 10.2 %collective-permute-start = (bf16[2,128,128]{2,1,0:T(8,128)(2,1)S(1)}, bf16[2,128,128]{2,1,0:T(8,128)(2,1)S(1)}, u32[]{:S(2)}, u32[]{:S(2)}) collective-permute-start(bf16[2,128,128]{2,1,0:T(8,128)(2,1)S(1)} %get-tuple-element.508), channel_id=1, source_target_pairs={{0,32},{32,64},{64,96},{96,128},{128,160},{160,192},{192,224},{224... | collective-permute-start | bytes 196616 | tf_op jit(solution)/shard_map/while/body/eval_jaxpr/ppermute | solution.py:15
  414.1 6.8 %collective-permute-start.1 = (bf16[2,128,128]{2,1,0:T(8,128)(2,1)S(1)}, bf16[2,128,128]{2,1,0:T(8,128)(2,1)S(1)}, u32[]{:S(2)}, u32[]{:S(2)}) collective-permute-start(bf16[2,128,128]{2,1,0:T(8,128)(2,1)S(1)} %get-tuple-element.509), channel_id=1, source_target_pairs={{0,32},{32,64},{64,96},{96,128},{128,160},{160,192},{192,224},{224... | collective-permute-start | bytes 196616 | tf_op jit(solution)/shard_map/while/body/eval_jaxpr/ppermute | solution.py:15
  422.6 9.6 %collective-permute-start = (bf16[2,128,128]{2,1,0:T(8,128)(2,1)S(1)}, bf16[2,128,128]{2,1,0:T(8,128)(2,1)S(1)}, u32[]{:S(2)}, u32[]{:S(2)}) collective-permute-start(bf16[2,128,128]{2,1,0:T(8,128)(2,1)S(1)} %get-tuple-element.508), channel_id=1, source_target_pairs={{0,32},{32,64},{64,96},{96,128},{128,160},{160,192},{192,224},{224... | collective-permute-start | bytes 196616 | tf_op jit(solution)/shard_map/while/body/eval_jaxpr/ppermute | solution.py:15
  430.2 6.4 %collective-permute-start.1 = (bf16[2,128,128]{2,1,0:T(8,128)(2,1)S(1)}, bf16[2,128,128]{2,1,0:T(8,128)(2,1)S(1)}, u32[]{:S(2)}, u32[]{:S(2)}) collective-permute-start(bf16[2,128,128]{2,1,0:T(8,128)(2,1)S(1)} %get-tuple-element.509), channel_id=1, source_target_pairs={{0,32},{32,64},{64,96},{96,128},{128,160},{160,192},{192,224},{224... | collective-permute-start | bytes 196616 | tf_op jit(solution)/shard_map/while/body/eval_jaxpr/ppermute | solution.py:15
  438.3 9.9 %collective-permute-start = (bf16[2,128,128]{2,1,0:T(8,128)(2,1)S(1)}, bf16[2,128,128]{2,1,0:T(8,128)(2,1)S(1)}, u32[]{:S(2)}, u32[]{:S(2)}) collective-permute-start(bf16[2,128,128]{2,1,0:T(8,128)(2,1)S(1)} %get-tuple-element.508), channel_id=1, source_target_pairs={{0,32},{32,64},{64,96},{96,128},{128,160},{160,192},{192,224},{224... | collective-permute-start | bytes 196616 | tf_op jit(solution)/shard_map/while/body/eval_jaxpr/ppermute | solution.py:15
  446.3 6.2 %collective-permute-start.1 = (bf16[2,128,128]{2,1,0:T(8,128)(2,1)S(1)}, bf16[2,128,128]{2,1,0:T(8,128)(2,1)S(1)}, u32[]{:S(2)}, u32[]{:S(2)}) collective-permute-start(bf16[2,128,128]{2,1,0:T(8,128)(2,1)S(1)} %get-tuple-element.509), channel_id=1, source_target_pairs={{0,32},{32,64},{64,96},{96,128},{128,160},{160,192},{192,224},{224... | collective-permute-start | bytes 196616 | tf_op jit(solution)/shard_map/while/body/eval_jaxpr/ppermute | solution.py:15
  452.5 11.8 %collective-permute-start = (bf16[2,128,128]{2,1,0:T(8,128)(2,1)S(1)}, bf16[2,128,128]{2,1,0:T(8,128)(2,1)S(1)}, u32[]{:S(2)}, u32[]{:S(2)}) collective-permute-start(bf16[2,128,128]{2,1,0:T(8,128)(2,1)S(1)} %get-tuple-element.508), channel_id=1, source_target_pairs={{0,32},{32,64},{64,96},{96,128},{128,160},{160,192},{192,224},{224... | collective-permute-start | bytes 196616 | tf_op jit(solution)/shard_map/while/body/eval_jaxpr/ppermute | solution.py:15
  462.3 6.2 %collective-permute-start.1 = (bf16[2,128,128]{2,1,0:T(8,128)(2,1)S(1)}, bf16[2,128,128]{2,1,0:T(8,128)(2,1)S(1)}, u32[]{:S(2)}, u32[]{:S(2)}) collective-permute-start(bf16[2,128,128]{2,1,0:T(8,128)(2,1)S(1)} %get-tuple-element.509), channel_id=1, source_target_pairs={{0,32},{32,64},{64,96},{96,128},{128,160},{160,192},{192,224},{224... | collective-permute-start | bytes 196616 | tf_op jit(solution)/shard_map/while/body/eval_jaxpr/ppermute | solution.py:15
  468.5 10.2 %collective-permute-start = (bf16[2,128,128]{2,1,0:T(8,128)(2,1)S(1)}, bf16[2,128,128]{2,1,0:T(8,128)(2,1)S(1)}, u32[]{:S(2)}, u32[]{:S(2)}) collective-permute-start(bf16[2,128,128]{2,1,0:T(8,128)(2,1)S(1)} %get-tuple-element.508), channel_id=1, source_target_pairs={{0,32},{32,64},{64,96},{96,128},{128,160},{160,192},{192,224},{224... | collective-permute-start | bytes 196616 | tf_op jit(solution)/shard_map/while/body/eval_jaxpr/ppermute | solution.py:15
  476.7 6.2 %collective-permute-start.1 = (bf16[2,128,128]{2,1,0:T(8,128)(2,1)S(1)}, bf16[2,128,128]{2,1,0:T(8,128)(2,1)S(1)}, u32[]{:S(2)}, u32[]{:S(2)}) collective-permute-start(bf16[2,128,128]{2,1,0:T(8,128)(2,1)S(1)} %get-tuple-element.509), channel_id=1, source_target_pairs={{0,32},{32,64},{64,96},{96,128},{128,160},{160,192},{192,224},{224... | collective-permute-start | bytes 196616 | tf_op jit(solution)/shard_map/while/body/eval_jaxpr/ppermute | solution.py:15
  482.9 11.0 %collective-permute-start = (bf16[2,128,128]{2,1,0:T(8,128)(2,1)S(1)}, bf16[2,128,128]{2,1,0:T(8,128)(2,1)S(1)}, u32[]{:S(2)}, u32[]{:S(2)}) collective-permute-start(bf16[2,128,128]{2,1,0:T(8,128)(2,1)S(1)} %get-tuple-element.508), channel_id=1, source_target_pairs={{0,32},{32,64},{64,96},{96,128},{128,160},{160,192},{192,224},{224... | collective-permute-start | bytes 196616 | tf_op jit(solution)/shard_map/while/body/eval_jaxpr/ppermute | solution.py:15
  492.0 6.4 %collective-permute-start.1 = (bf16[2,128,128]{2,1,0:T(8,128)(2,1)S(1)}, bf16[2,128,128]{2,1,0:T(8,128)(2,1)S(1)}, u32[]{:S(2)}, u32[]{:S(2)}) collective-permute-start(bf16[2,128,128]{2,1,0:T(8,128)(2,1)S(1)} %get-tuple-element.509), channel_id=1, source_target_pairs={{0,32},{32,64},{64,96},{96,128},{128,160},{160,192},{192,224},{224... | collective-permute-start | bytes 196616 | tf_op jit(solution)/shard_map/while/body/eval_jaxpr/ppermute | solution.py:15
  498.4 11.3 %collective-permute-start = (bf16[2,128,128]{2,1,0:T(8,128)(2,1)S(1)}, bf16[2,128,128]{2,1,0:T(8,128)(2,1)S(1)}, u32[]{:S(2)}, u32[]{:S(2)}) collective-permute-start(bf16[2,128,128]{2,1,0:T(8,128)(2,1)S(1)} %get-tuple-element.508), channel_id=1, source_target_pairs={{0,32},{32,64},{64,96},{96,128},{128,160},{160,192},{192,224},{224... | collective-permute-start | bytes 196616 | tf_op jit(solution)/shard_map/while/body/eval_jaxpr/ppermute | solution.py:15
  507.4 6.4 %collective-permute-start.1 = (bf16[2,128,128]{2,1,0:T(8,128)(2,1)S(1)}, bf16[2,128,128]{2,1,0:T(8,128)(2,1)S(1)}, u32[]{:S(2)}, u32[]{:S(2)}) collective-permute-start(bf16[2,128,128]{2,1,0:T(8,128)(2,1)S(1)} %get-tuple-element.509), channel_id=1, source_target_pairs={{0,32},{32,64},{64,96},{96,128},{128,160},{160,192},{192,224},{224... | collective-permute-start | bytes 196616 | tf_op jit(solution)/shard_map/while/body/eval_jaxpr/ppermute | solution.py:15
  513.9 11.5 %collective-permute-start = (bf16[2,128,128]{2,1,0:T(8,128)(2,1)S(1)}, bf16[2,128,128]{2,1,0:T(8,128)(2,1)S(1)}, u32[]{:S(2)}, u32[]{:S(2)}) collective-permute-start(bf16[2,128,128]{2,1,0:T(8,128)(2,1)S(1)} %get-tuple-element.508), channel_id=1, source_target_pairs={{0,32},{32,64},{64,96},{96,128},{128,160},{160,192},{192,224},{224... | collective-permute-start | bytes 196616 | tf_op jit(solution)/shard_map/while/body/eval_jaxpr/ppermute | solution.py:15
  523.5 6.2 %collective-permute-start.1 = (bf16[2,128,128]{2,1,0:T(8,128)(2,1)S(1)}, bf16[2,128,128]{2,1,0:T(8,128)(2,1)S(1)}, u32[]{:S(2)}, u32[]{:S(2)}) collective-permute-start(bf16[2,128,128]{2,1,0:T(8,128)(2,1)S(1)} %get-tuple-element.509), channel_id=1, source_target_pairs={{0,32},{32,64},{64,96},{96,128},{128,160},{160,192},{192,224},{224... | collective-permute-start | bytes 196616 | tf_op jit(solution)/shard_map/while/body/eval_jaxpr/ppermute | solution.py:15
  529.7 11.2 %collective-permute-start = (bf16[2,128,128]{2,1,0:T(8,128)(2,1)S(1)}, bf16[2,128,128]{2,1,0:T(8,128)(2,1)S(1)}, u32[]{:S(2)}, u32[]{:S(2)}) collective-permute-start(bf16[2,128,128]{2,1,0:T(8,128)(2,1)S(1)} %get-tuple-element.508), channel_id=1, source_target_pairs={{0,32},{32,64},{64,96},{96,128},{128,160},{160,192},{192,224},{224... | collective-permute-start | bytes 196616 | tf_op jit(solution)/shard_map/while/body/eval_jaxpr/ppermute | solution.py:15
  538.5 6.2 %collective-permute-start.1 = (bf16[2,128,128]{2,1,0:T(8,128)(2,1)S(1)}, bf16[2,128,128]{2,1,0:T(8,128)(2,1)S(1)}, u32[]{:S(2)}, u32[]{:S(2)}) collective-permute-start(bf16[2,128,128]{2,1,0:T(8,128)(2,1)S(1)} %get-tuple-element.509), channel_id=1, source_target_pairs={{0,32},{32,64},{64,96},{96,128},{128,160},{160,192},{192,224},{224... | collective-permute-start | bytes 196616 | tf_op jit(solution)/shard_map/while/body/eval_jaxpr/ppermute | solution.py:15
  544.7 10.5 %collective-permute-start = (bf16[2,128,128]{2,1,0:T(8,128)(2,1)S(1)}, bf16[2,128,128]{2,1,0:T(8,128)(2,1)S(1)}, u32[]{:S(2)}, u32[]{:S(2)}) collective-permute-start(bf16[2,128,128]{2,1,0:T(8,128)(2,1)S(1)} %get-tuple-element.508), channel_id=1, source_target_pairs={{0,32},{32,64},{64,96},{96,128},{128,160},{160,192},{192,224},{224... | collective-permute-start | bytes 196616 | tf_op jit(solution)/shard_map/while/body/eval_jaxpr/ppermute | solution.py:15
  553.2 6.2 %collective-permute-start.1 = (bf16[2,128,128]{2,1,0:T(8,128)(2,1)S(1)}, bf16[2,128,128]{2,1,0:T(8,128)(2,1)S(1)}, u32[]{:S(2)}, u32[]{:S(2)}) collective-permute-start(bf16[2,128,128]{2,1,0:T(8,128)(2,1)S(1)} %get-tuple-element.509), channel_id=1, source_target_pairs={{0,32},{32,64},{64,96},{96,128},{128,160},{160,192},{192,224},{224... | collective-permute-start | bytes 196616 | tf_op jit(solution)/shard_map/while/body/eval_jaxpr/ppermute | solution.py:15
Sparse Core Ops, SparseCore 0:
  11.2 95.8 all-gather.3
  110.3 103.0 all-gather.5
  216.4 94.1 all-gather.7
where the time goes:
time: 574 us; the launch traced here: 572 us
  waiting for transfers between devices  335 us (58%)
  starting transfers between devices  173 us (30%)
  matrix products  20.2 us (4%)
  local copies, waits for them, and re-layouts  15.1 us (3%)
  between operations  14.1 us (2%)
  other arithmetic  14 us (2%)
    ppermute x30, starting transfers between devices, passed_along(): return lax.ppermute(block, axis, route)  157 us
    all_gather x1, waiting for transfers between devices, shards(): up_piece = lax.all_gather(w_up, 'ctx', axis=1, tiled=True)  103 us
    all_gather x1, waiting for transfers between devices, shards(): lax.all_gather(w_down, 'ctx', axis=2, tiled=True)[0]  97.3 us
    all_to_all x1, waiting for transfers between devices, shards(): lax.all_to_all(outgoing.reshape(owners, CAP, width), 'dp', split_axis=0,...  64.5 us
    ppermute x30, waiting for transfers between devices, passed_along(): return lax.ppermute(block, axis, route)  63.6 us
  transfers between devices with their start and end apart: 35, of which 21 were waited for; matrix products, arithmetic and copies ran while one was open for 6% of the time, Pallas kernels for 0%

commit v1 on v0

--- a/solution.py
+++ b/solution.py
@@ -111,8 +111,11 @@
     arrived = lax.all_to_all(
         outgoing.reshape(owners, CAP, width), "dp", split_axis=0, concat_axis=0, tiled=True
     ).reshape(slots, width)
-    gate_piece = lax.all_gather(w_gate, "ctx", axis=1, tiled=True)
-    up_piece = lax.all_gather(w_up, "ctx", axis=1, tiled=True)
+    gate_piece, up_piece = jnp.split(
+        lax.all_gather(jnp.concatenate([w_gate, w_up], axis=0), "ctx", axis=1, tiled=True),
+        [w_gate.shape[0]],
+        axis=0,
+    )
     gate_sum = jnp.dot(arrived, gate_piece[0], preferred_element_type=jnp.float32)
     up_sum = jnp.dot(arrived, up_piece[0], preferred_element_type=jnp.float32)
     hidden = (jax.nn.silu(gate_sum) * up_sum).astype(jnp.bfloat16)

time: 574 us -> 501 us (0.87)
  waiting for transfers between devices: 335 us -> 261 us
    all_gather x2 -> x1, waiting for transfers between devices: 107 us -> 4.34 us  [shards(): lax.all_gather(jnp.concatenate([w_gate, w_up], axis=0), 'ctx', axis=1, ti...]
    all_to_all x1, waiting for transfers between devices: 64.5 us -> 83.6 us  [shards(): lax.all_to_all(outgoing.reshape(owners, CAP, width), 'dp', split_axis=0,...]
    all_gather x1, waiting for transfers between devices: 97.3 us -> 108 us  [shards(): lax.all_gather(w_down, 'ctx', axis=2, tiled=True)[0]]
  transfers between devices with their start and end apart: 35 -> 34, of which waited for: 21 -> 20; matrix products, arithmetic and copies ran while one was open for 6% -> 7% of each run, Pallas kernels for 0% -> 0%
where the time goes in v1:
time: 501 us; the launch traced here: 500 us
  waiting for transfers between devices  261 us (52%)
  starting transfers between devices  172 us (34%)
  matrix products  20.2 us (4%)
  other arithmetic  15.7 us (3%)
  local copies, waits for them, and re-layouts  15.2 us (3%)
  between operations  14.4 us (3%)
    ppermute x30, starting transfers between devices, passed_along(): return lax.ppermute(block, axis, route)  156 us
    all_gather x1, waiting for transfers between devices, shards(): lax.all_gather(w_down, 'ctx', axis=2, tiled=True)[0]  108 us
    all_to_all x1, waiting for transfers between devices, shards(): lax.all_to_all(outgoing.reshape(owners, CAP, width), 'dp', split_axis=0,...  83.6 us
    ppermute x30, waiting for transfers between devices, passed_along(): return lax.ppermute(block, axis, route)  63.9 us
    all_to_all x1, starting transfers between devices, shards(): lax.all_to_all(outgoing.reshape(owners, CAP, width), 'dp', split_axis=0,...  10.5 us
  transfers between devices with their start and end apart: 34, of which 20 were waited for; matrix products, arithmetic and copies ran while one was open for 7% of the time, Pallas kernels for 0%

profile of v1, /device:TPU:62, one launch (start us, length us, event | category | flops | bytes accessed | tf_op | source)
XLA Modules:
  0.0 500.1 jit_solution(16648692425954396788)
XLA Ops:
  7.2 1.7 pad_maximum_fusion
  9.9 9.0 %reduce-window.6 = s32[32,8,128]{2,1,0:T(8,128)S(1)} reduce-window(s32[32,8,128]{2,1,0:T(8,128)S(1)} %fusion.41, s32[]{:T(128)} %constant.106.clone.1), window={size=1x1x128 pad=0_0x0_0x127_0}, to_apply=%region_8.9 | reduce-window | flops 4161536 | bytes 262148 | tf_op jit(solution)/shard_map/reduce-window
  22.5 10.5 %all-to-all-start = ((bf16[32,12,2048]{2,1,0:T(8,128)(2,1)}), bf16[32,12,2048]{2,1,0:T(8,128)(2,1)}, u32[]{:S(2)}, u32[]{:S(2)}) async-start(bf16[32,12,2048]{2,1,0:T(8,128)(2,1)} %reshape.192), calls=%async_computation | async-start | bytes 4194304 | tf_op jit(solution)/shard_map/all_to_all | solution.py:111
  35.5 83.6 %all-to-all-done = bf16[32,12,2048]{2,1,0:T(8,128)(2,1)} async-done(((bf16[32,12,2048]{2,1,0:T(8,128)(2,1)}), bf16[32,12,2048]{2,1,0:T(8,128)(2,1)}, u32[]{:S(2)}, u32[]{:S(2)}) %all-to-all-start) | async-done | bytes 1572896 | tf_op jit(solution)/shard_map/all_to_all | solution.py:111
  119.1 3.6 reshape.193
  122.8 4.3 all-gather.3.cloned.1.call-done
  127.1 2.8 fusion.14
  130.0 107.9 %all-gather.5.cloned.1.call-done = bf16[1,384,2048]{2,1,0:T(8,128)(2,1)} async-done(((bf16[1,384,128]{2,1,0:T(8,128)(2,1)}), bf16[1,384,2048]{2,1,0:T(8,128)(2,1)}) %all-gather.5.cloned.1.call-update) | async-done | bytes 1572880 | tf_op jit(solution)/shard_map/all_gather | solution.py:124
  237.9 5.4 %convolution_convert_fusion = bf16[384,2048]{1,0:T(8,128)(2,1)} fusion(bf16[1,384,2048]{2,1,0:T(8,128)(2,1)} %all-gather.5.cloned.1.call-done, bf16[384,2048]{1,0:T(8,128)(2,1)} %reshape.193, bf16[2,2048,384]{2,1,0:T(8,128)(2,1)} %all-gather.3.cloned.1.call-done, f32[384,384]{1,0:T(8,128)S(1)} %fusion.14), kind=kOutput, calls=%fused_computation.21 | convolution fusion | flops 1209630720 | bytes 6881280 | tf_op jit(solution)/shard_map/dot_general | solution.py:122
  243.2 3.6 reshape.194
  246.9 5.4 %all-to-all-start.1 = ((bf16[32,12,2048]{2,1,0:T(8,128)(2,1)}), bf16[32,12,2048]{2,1,0:T(8,128)(2,1)}, u32[]{:S(2)}, u32[]{:S(2)}) async-start(bf16[32,12,2048]{2,1,0:T(8,128)(2,1)} %reshape.194), calls=%async_computation.1 | async-start | bytes 4194304 | tf_op jit(solution)/shard_map/all_to_all | solution.py:128
  253.3 233.5 %while.24 = (s32[]{:T(128)}, f32[2,1024]{1,0:T(2,128)S(1)}, f32[2,1024]{1,0:T(2,128)S(1)}, f32[2,1024,128]{2,1,0:T(8,128)S(1)}, bf16[2,128,128]{2,1,0:T(8,128)(2...) while((s32[]{:T(128)}, f32[2,1024]{1,0:T(2,128)S(1)}, ...), condition=%wide.region_7.8_spmd.clone, body=%wide.region_2.7_spmd.clone.sunk | while | flops 137243792 | bytes 7378492 | solution.py:84
  253.4 4.6 collective-permute-start
  258.0 2.5 collective-permute-start.1
  260.6 3.6 collective-permute-done.1
  264.2 1.6 conditional.3
  265.9 10.2 %collective-permute-start = (bf16[2,128,128]{2,1,0:T(8,128)(2,1)S(1)}, bf16[2,128,128]{2,1,0:T(8,128)(2,1)S(1)}, u32[]{:S(2)}, u32[]{:S(2)}) collective-permute-start(bf16[2,128,128]{2,1,0:T(8,128)(2,1)S(1)} %get-tuple-element.508), channel_id=1, source_target_pairs={{0,32},{32,64},{64,96},{96,128},{128,160},{160,192},{192,224},{224... | collective-permute-start | bytes 196616 | tf_op jit(solution)/shard_map/while/body/eval_jaxpr/ppermute | solution.py:15
  276.1 1.9 collective-permute-start.1
  278.1 4.2 collective-permute-done.1
  282.2 1.6 conditional.3
  283.9 8.7 %collective-permute-start = (bf16[2,128,128]{2,1,0:T(8,128)(2,1)S(1)}, bf16[2,128,128]{2,1,0:T(8,128)(2,1)S(1)}, u32[]{:S(2)}, u32[]{:S(2)}) collective-permute-start(bf16[2,128,128]{2,1,0:T(8,128)(2,1)S(1)} %get-tuple-element.508), channel_id=1, source_target_pairs={{0,32},{32,64},{64,96},{96,128},{128,160},{160,192},{192,224},{224... | collective-permute-start | bytes 196616 | tf_op jit(solution)/shard_map/while/body/eval_jaxpr/ppermute | solution.py:15
  292.7 1.9 collective-permute-start.1
  294.6 4.2 collective-permute-done.1
  298.8 1.6 conditional.3
  300.5 8.7 %collective-permute-start = (bf16[2,128,128]{2,1,0:T(8,128)(2,1)S(1)}, bf16[2,128,128]{2,1,0:T(8,128)(2,1)S(1)}, u32[]{:S(2)}, u32[]{:S(2)}) collective-permute-start(bf16[2,128,128]{2,1,0:T(8,128)(2,1)S(1)} %get-tuple-element.508), channel_id=1, source_target_pairs={{0,32},{32,64},{64,96},{96,128},{128,160},{160,192},{192,224},{224... | collective-permute-start | bytes 196616 | tf_op jit(solution)/shard_map/while/body/eval_jaxpr/ppermute | solution.py:15
  309.2 1.9 collective-permute-start.1
  311.2 4.2 collective-permute-done.1
  315.4 1.6 conditional.3
  317.1 8.2 %collective-permute-start = (bf16[2,128,128]{2,1,0:T(8,128)(2,1)S(1)}, bf16[2,128,128]{2,1,0:T(8,128)(2,1)S(1)}, u32[]{:S(2)}, u32[]{:S(2)}) collective-permute-start(bf16[2,128,128]{2,1,0:T(8,128)(2,1)S(1)} %get-tuple-element.508), channel_id=1, source_target_pairs={{0,32},{32,64},{64,96},{96,128},{128,160},{160,192},{192,224},{224... | collective-permute-start | bytes 196616 | tf_op jit(solution)/shard_map/while/body/eval_jaxpr/ppermute | solution.py:15
  325.3 1.9 collective-permute-start.1
  327.3 4.2 collective-permute-done.1
  331.5 1.6 conditional.3
  333.1 8.2 %collective-permute-start = (bf16[2,128,128]{2,1,0:T(8,128)(2,1)S(1)}, bf16[2,128,128]{2,1,0:T(8,128)(2,1)S(1)}, u32[]{:S(2)}, u32[]{:S(2)}) collective-permute-start(bf16[2,128,128]{2,1,0:T(8,128)(2,1)S(1)} %get-tuple-element.508), channel_id=1, source_target_pairs={{0,32},{32,64},{64,96},{96,128},{128,160},{160,192},{192,224},{224... | collective-permute-start | bytes 196616 | tf_op jit(solution)/shard_map/while/body/eval_jaxpr/ppermute | solution.py:15
  341.3 1.9 collective-permute-start.1
  343.3 4.9 collective-permute-done.1
  349.9 7.5 %collective-permute-start = (bf16[2,128,128]{2,1,0:T(8,128)(2,1)S(1)}, bf16[2,128,128]{2,1,0:T(8,128)(2,1)S(1)}, u32[]{:S(2)}, u32[]{:S(2)}) collective-permute-start(bf16[2,128,128]{2,1,0:T(8,128)(2,1)S(1)} %get-tuple-element.508), channel_id=1, source_target_pairs={{0,32},{32,64},{64,96},{96,128},{128,160},{160,192},{192,224},{224... | collective-permute-start | bytes 196616 | tf_op jit(solution)/shard_map/while/body/eval_jaxpr/ppermute | solution.py:15
  357.4 1.9 collective-permute-start.1
  359.4 4.6 collective-permute-done.1
  363.9 1.6 conditional.3
  365.6 7.8 %collective-permute-start = (bf16[2,128,128]{2,1,0:T(8,128)(2,1)S(1)}, bf16[2,128,128]{2,1,0:T(8,128)(2,1)S(1)}, u32[]{:S(2)}, u32[]{:S(2)}) collective-permute-start(bf16[2,128,128]{2,1,0:T(8,128)(2,1)S(1)} %get-tuple-element.508), channel_id=1, source_target_pairs={{0,32},{32,64},{64,96},{96,128},{128,160},{160,192},{192,224},{224... | collective-permute-start | bytes 196616 | tf_op jit(solution)/shard_map/while/body/eval_jaxpr/ppermute | solution.py:15
  373.4 1.9 collective-permute-start.1
  375.4 4.2 collective-permute-done.1
  379.6 9.8 %collective-permute-start = (bf16[2,128,128]{2,1,0:T(8,128)(2,1)S(1)}, bf16[2,128,128]{2,1,0:T(8,128)(2,1)S(1)}, u32[]{:S(2)}, u32[]{:S(2)}) collective-permute-start(bf16[2,128,128]{2,1,0:T(8,128)(2,1)S(1)} %get-tuple-element.508), channel_id=1, source_target_pairs={{0,32},{32,64},{64,96},{96,128},{128,160},{160,192},{192,224},{224... | collective-permute-start | bytes 196616 | tf_op jit(solution)/shard_map/while/body/eval_jaxpr/ppermute | solution.py:15
  389.5 1.9 collective-permute-start.1
  391.4 4.2 collective-permute-done.1
  395.7 8.2 %collective-permute-start = (bf16[2,128,128]{2,1,0:T(8,128)(2,1)S(1)}, bf16[2,128,128]{2,1,0:T(8,128)(2,1)S(1)}, u32[]{:S(2)}, u32[]{:S(2)}) collective-permute-start(bf16[2,128,128]{2,1,0:T(8,128)(2,1)S(1)} %get-tuple-element.508), channel_id=1, source_target_pairs={{0,32},{32,64},{64,96},{96,128},{128,160},{160,192},{192,224},{224... | collective-permute-start | bytes 196616 | tf_op jit(solution)/shard_map/while/body/eval_jaxpr/ppermute | solution.py:15
  403.8 1.9 collective-permute-start.1
  405.8 4.2 collective-permute-done.1
  410.0 8.4 %collective-permute-start = (bf16[2,128,128]{2,1,0:T(8,128)(2,1)S(1)}, bf16[2,128,128]{2,1,0:T(8,128)(2,1)S(1)}, u32[]{:S(2)}, u32[]{:S(2)}) collective-permute-start(bf16[2,128,128]{2,1,0:T(8,128)(2,1)S(1)} %get-tuple-element.508), channel_id=1, source_target_pairs={{0,32},{32,64},{64,96},{96,128},{128,160},{160,192},{192,224},{224... | collective-permute-start | bytes 196616 | tf_op jit(solution)/shard_map/while/body/eval_jaxpr/ppermute | solution.py:15
  418.4 1.9 collective-permute-start.1
  420.4 4.2 collective-permute-done.1
  424.6 9.3 %collective-permute-start = (bf16[2,128,128]{2,1,0:T(8,128)(2,1)S(1)}, bf16[2,128,128]{2,1,0:T(8,128)(2,1)S(1)}, u32[]{:S(2)}, u32[]{:S(2)}) collective-permute-start(bf16[2,128,128]{2,1,0:T(8,128)(2,1)S(1)} %get-tuple-element.508), channel_id=1, source_target_pairs={{0,32},{32,64},{64,96},{96,128},{128,160},{160,192},{192,224},{224... | collective-permute-start | bytes 196616 | tf_op jit(solution)/shard_map/while/body/eval_jaxpr/ppermute | solution.py:15
  433.9 1.9 collective-permute-start.1
  436.2 4.6 collective-permute-done.1
  440.8 9.6 %collective-permute-start = (bf16[2,128,128]{2,1,0:T(8,128)(2,1)S(1)}, bf16[2,128,128]{2,1,0:T(8,128)(2,1)S(1)}, u32[]{:S(2)}, u32[]{:S(2)}) collective-permute-start(bf16[2,128,128]{2,1,0:T(8,128)(2,1)S(1)} %get-tuple-element.508), channel_id=1, source_target_pairs={{0,32},{32,64},{64,96},{96,128},{128,160},{160,192},{192,224},{224... | collective-permute-start | bytes 196616 | tf_op jit(solution)/shard_map/while/body/eval_jaxpr/ppermute | solution.py:15
  450.4 1.9 collective-permute-start.1
  452.4 4.2 collective-permute-done.1
  456.6 9.4 %collective-permute-start = (bf16[2,128,128]{2,1,0:T(8,128)(2,1)S(1)}, bf16[2,128,128]{2,1,0:T(8,128)(2,1)S(1)}, u32[]{:S(2)}, u32[]{:S(2)}) collective-permute-start(bf16[2,128,128]{2,1,0:T(8,128)(2,1)S(1)} %get-tuple-element.508), channel_id=1, source_target_pairs={{0,32},{32,64},{64,96},{96,128},{128,160},{160,192},{192,224},{224... | collective-permute-start | bytes 196616 | tf_op jit(solution)/shard_map/while/body/eval_jaxpr/ppermute | solution.py:15
  466.0 1.9 collective-permute-start.1
  468.4 3.8 collective-permute-done.1
  472.2 8.4 %collective-permute-start = (bf16[2,128,128]{2,1,0:T(8,128)(2,1)S(1)}, bf16[2,128,128]{2,1,0:T(8,128)(2,1)S(1)}, u32[]{:S(2)}, u32[]{:S(2)}) collective-permute-start(bf16[2,128,128]{2,1,0:T(8,128)(2,1)S(1)} %get-tuple-element.508), channel_id=1, source_target_pairs={{0,32},{32,64},{64,96},{96,128},{128,160},{160,192},{192,224},{224... | collective-permute-start | bytes 196616 | tf_op jit(solution)/shard_map/while/body/eval_jaxpr/ppermute | solution.py:15
  480.6 1.9 collective-permute-start.1
  482.6 4.2 collective-permute-done.1
  488.9 2.5 reshape.197
  (205 shorter events, 25.6 us)
Async XLA Ops:
  7.2 12.9 %copy-start = (bf16[1,128,2048]{2,1,0:T(8,128)(2,1)S(1)}, bf16[1,128,2048]{2,1,0:T(8,128)(2,1)}, u32[]{:S(2)}) copy-start(bf16[1,128,2048]{2,1,0:T(8,128)(2,1)} %param.17) | copy-start | bytes 1572868
  7.2 13.1 %copy-start.4 = (f32[2048]{0:T(1024)S(1)}, f32[2048]{0:T(1024)}, u32[]{:S(2)}) copy-start(f32[2048]{0:T(1024)} %param.18) | copy-start | bytes 24580
  7.2 119.9 %all-gather.3.cloned.1.call-start = ((), (), s32[]{:S(2)}) async-start(), calls=%async_computation.2 | async-start | bytes 3342336 | tf_op jit(solution)/shard_map/all_gather | solution.py:115
  22.5 11.3 %copy-start.5 = (f32[1,128,8]{1,2,0:T(8,128)S(1)}, f32[1,128,8]{1,2,0:T(8,128)}, u32[]{:S(2)}) copy-start(f32[1,128,8]{1,2,0:T(8,128)} %param.20) | copy-start | bytes 12292
  22.5 11.5 %copy-start.1 = (bf16[1,128,2048]{2,1,0:T(8,128)(2,1)S(1)}, bf16[1,128,2048]{2,1,0:T(8,128)(2,1)}, u32[]{:S(2)}) copy-start(bf16[1,128,2048]{2,1,0:T(8,128)(2,1)} %param.14) | copy-start | bytes 1572868
  22.5 96.6 %all-to-all-start = ((bf16[32,12,2048]{2,1,0:T(8,128)(2,1)}), bf16[32,12,2048]{2,1,0:T(8,128)(2,1)}, u32[]{:S(2)}, u32[]{:S(2)}) async-start(bf16[32,12,2048]{2,1,0:T(8,128)(2,1)} %reshape.192), calls=%async_computation | async-start | bytes 4194304 | tf_op jit(solution)/shard_map/all_to_all | solution.py:111
  33.1 1.3 copy-start.2
  33.1 1.4 copy-start.3
  33.1 204.8 %all-gather.5.cloned.1.call-start = ((), (), s32[]{:S(2)}) async-start(), calls=%async_computation.3 | async-start | bytes 1671168 | tf_op jit(solution)/shard_map/all_gather | solution.py:124
  246.9 242.0 %all-to-all-start.1 = ((bf16[32,12,2048]{2,1,0:T(8,128)(2,1)}), bf16[32,12,2048]{2,1,0:T(8,128)(2,1)}, u32[]{:S(2)}, u32[]{:S(2)}) async-start(bf16[32,12,2048]{2,1,0:T(8,128)(2,1)} %reshape.194), calls=%async_computation.1 | async-start | bytes 4194304 | tf_op jit(solution)/shard_map/all_to_all | solution.py:128
  253.4 7.2 %collective-permute-start = (bf16[2,128,128]{2,1,0:T(8,128)(2,1)S(1)}, bf16[2,128,128]{2,1,0:T(8,128)(2,1)S(1)}, u32[]{:S(2)}, u32[]{:S(2)}) collective-permute-start(bf16[2,128,128]{2,1,0:T(8,128)(2,1)S(1)} %get-tuple-element.508), channel_id=1, source_target_pairs={{0,32},{32,64},{64,96},{96,128},{128,160},{160,192},{192,224},{224... | collective-permute-start | bytes 196616 | tf_op jit(solution)/shard_map/while/body/eval_jaxpr/ppermute | solution.py:15
  258.0 6.2 %collective-permute-start.1 = (bf16[2,128,128]{2,1,0:T(8,128)(2,1)S(1)}, bf16[2,128,128]{2,1,0:T(8,128)(2,1)S(1)}, u32[]{:S(2)}, u32[]{:S(2)}) collective-permute-start(bf16[2,128,128]{2,1,0:T(8,128)(2,1)S(1)} %get-tuple-element.509), channel_id=1, source_target_pairs={{0,32},{32,64},{64,96},{96,128},{128,160},{160,192},{192,224},{224... | collective-permute-start | bytes 196616 | tf_op jit(solution)/shard_map/while/body/eval_jaxpr/ppermute | solution.py:15
  265.9 12.2 %collective-permute-start = (bf16[2,128,128]{2,1,0:T(8,128)(2,1)S(1)}, bf16[2,128,128]{2,1,0:T(8,128)(2,1)S(1)}, u32[]{:S(2)}, u32[]{:S(2)}) collective-permute-start(bf16[2,128,128]{2,1,0:T(8,128)(2,1)S(1)} %get-tuple-element.508), channel_id=1, source_target_pairs={{0,32},{32,64},{64,96},{96,128},{128,160},{160,192},{192,224},{224... | collective-permute-start | bytes 196616 | tf_op jit(solution)/shard_map/while/body/eval_jaxpr/ppermute | solution.py:15
  276.1 6.2 %collective-permute-start.1 = (bf16[2,128,128]{2,1,0:T(8,128)(2,1)S(1)}, bf16[2,128,128]{2,1,0:T(8,128)(2,1)S(1)}, u32[]{:S(2)}, u32[]{:S(2)}) collective-permute-start(bf16[2,128,128]{2,1,0:T(8,128)(2,1)S(1)} %get-tuple-element.509), channel_id=1, source_target_pairs={{0,32},{32,64},{64,96},{96,128},{128,160},{160,192},{192,224},{224... | collective-permute-start | bytes 196616 | tf_op jit(solution)/shard_map/while/body/eval_jaxpr/ppermute | solution.py:15
  283.9 10.7 %collective-permute-start = (bf16[2,128,128]{2,1,0:T(8,128)(2,1)S(1)}, bf16[2,128,128]{2,1,0:T(8,128)(2,1)S(1)}, u32[]{:S(2)}, u32[]{:S(2)}) collective-permute-start(bf16[2,128,128]{2,1,0:T(8,128)(2,1)S(1)} %get-tuple-element.508), channel_id=1, source_target_pairs={{0,32},{32,64},{64,96},{96,128},{128,160},{160,192},{192,224},{224... | collective-permute-start | bytes 196616 | tf_op jit(solution)/shard_map/while/body/eval_jaxpr/ppermute | solution.py:15
  292.7 6.2 %collective-permute-start.1 = (bf16[2,128,128]{2,1,0:T(8,128)(2,1)S(1)}, bf16[2,128,128]{2,1,0:T(8,128)(2,1)S(1)}, u32[]{:S(2)}, u32[]{:S(2)}) collective-permute-start(bf16[2,128,128]{2,1,0:T(8,128)(2,1)S(1)} %get-tuple-element.509), channel_id=1, source_target_pairs={{0,32},{32,64},{64,96},{96,128},{128,160},{160,192},{192,224},{224... | collective-permute-start | bytes 196616 | tf_op jit(solution)/shard_map/while/body/eval_jaxpr/ppermute | solution.py:15
  300.5 10.7 %collective-permute-start = (bf16[2,128,128]{2,1,0:T(8,128)(2,1)S(1)}, bf16[2,128,128]{2,1,0:T(8,128)(2,1)S(1)}, u32[]{:S(2)}, u32[]{:S(2)}) collective-permute-start(bf16[2,128,128]{2,1,0:T(8,128)(2,1)S(1)} %get-tuple-element.508), channel_id=1, source_target_pairs={{0,32},{32,64},{64,96},{96,128},{128,160},{160,192},{192,224},{224... | collective-permute-start | bytes 196616 | tf_op jit(solution)/shard_map/while/body/eval_jaxpr/ppermute | solution.py:15
  309.2 6.2 %collective-permute-start.1 = (bf16[2,128,128]{2,1,0:T(8,128)(2,1)S(1)}, bf16[2,128,128]{2,1,0:T(8,128)(2,1)S(1)}, u32[]{:S(2)}, u32[]{:S(2)}) collective-permute-start(bf16[2,128,128]{2,1,0:T(8,128)(2,1)S(1)} %get-tuple-element.509), channel_id=1, source_target_pairs={{0,32},{32,64},{64,96},{96,128},{128,160},{160,192},{192,224},{224... | collective-permute-start | bytes 196616 | tf_op jit(solution)/shard_map/while/body/eval_jaxpr/ppermute | solution.py:15
  317.1 10.2 %collective-permute-start = (bf16[2,128,128]{2,1,0:T(8,128)(2,1)S(1)}, bf16[2,128,128]{2,1,0:T(8,128)(2,1)S(1)}, u32[]{:S(2)}, u32[]{:S(2)}) collective-permute-start(bf16[2,128,128]{2,1,0:T(8,128)(2,1)S(1)} %get-tuple-element.508), channel_id=1, source_target_pairs={{0,32},{32,64},{64,96},{96,128},{128,160},{160,192},{192,224},{224... | collective-permute-start | bytes 196616 | tf_op jit(solution)/shard_map/while/body/eval_jaxpr/ppermute | solution.py:15
  325.3 6.2 %collective-permute-start.1 = (bf16[2,128,128]{2,1,0:T(8,128)(2,1)S(1)}, bf16[2,128,128]{2,1,0:T(8,128)(2,1)S(1)}, u32[]{:S(2)}, u32[]{:S(2)}) collective-permute-start(bf16[2,128,128]{2,1,0:T(8,128)(2,1)S(1)} %get-tuple-element.509), channel_id=1, source_target_pairs={{0,32},{32,64},{64,96},{96,128},{128,160},{160,192},{192,224},{224... | collective-permute-start | bytes 196616 | tf_op jit(solution)/shard_map/while/body/eval_jaxpr/ppermute | solution.py:15
  333.1 10.2 %collective-permute-start = (bf16[2,128,128]{2,1,0:T(8,128)(2,1)S(1)}, bf16[2,128,128]{2,1,0:T(8,128)(2,1)S(1)}, u32[]{:S(2)}, u32[]{:S(2)}) collective-permute-start(bf16[2,128,128]{2,1,0:T(8,128)(2,1)S(1)} %get-tuple-element.508), channel_id=1, source_target_pairs={{0,32},{32,64},{64,96},{96,128},{128,160},{160,192},{192,224},{224... | collective-permute-start | bytes 196616 | tf_op jit(solution)/shard_map/while/body/eval_jaxpr/ppermute | solution.py:15
  341.3 6.9 %collective-permute-start.1 = (bf16[2,128,128]{2,1,0:T(8,128)(2,1)S(1)}, bf16[2,128,128]{2,1,0:T(8,128)(2,1)S(1)}, u32[]{:S(2)}, u32[]{:S(2)}) collective-permute-start(bf16[2,128,128]{2,1,0:T(8,128)(2,1)S(1)} %get-tuple-element.509), channel_id=1, source_target_pairs={{0,32},{32,64},{64,96},{96,128},{128,160},{160,192},{192,224},{224... | collective-permute-start | bytes 196616 | tf_op jit(solution)/shard_map/while/body/eval_jaxpr/ppermute | solution.py:15
  349.9 9.5 %collective-permute-start = (bf16[2,128,128]{2,1,0:T(8,128)(2,1)S(1)}, bf16[2,128,128]{2,1,0:T(8,128)(2,1)S(1)}, u32[]{:S(2)}, u32[]{:S(2)}) collective-permute-start(bf16[2,128,128]{2,1,0:T(8,128)(2,1)S(1)} %get-tuple-element.508), channel_id=1, source_target_pairs={{0,32},{32,64},{64,96},{96,128},{128,160},{160,192},{192,224},{224... | collective-permute-start | bytes 196616 | tf_op jit(solution)/shard_map/while/body/eval_jaxpr/ppermute | solution.py:15
  357.4 6.5 %collective-permute-start.1 = (bf16[2,128,128]{2,1,0:T(8,128)(2,1)S(1)}, bf16[2,128,128]{2,1,0:T(8,128)(2,1)S(1)}, u32[]{:S(2)}, u32[]{:S(2)}) collective-permute-start(bf16[2,128,128]{2,1,0:T(8,128)(2,1)S(1)} %get-tuple-element.509), channel_id=1, source_target_pairs={{0,32},{32,64},{64,96},{96,128},{128,160},{160,192},{192,224},{224... | collective-permute-start | bytes 196616 | tf_op jit(solution)/shard_map/while/body/eval_jaxpr/ppermute | solution.py:15
  365.6 9.8 %collective-permute-start = (bf16[2,128,128]{2,1,0:T(8,128)(2,1)S(1)}, bf16[2,128,128]{2,1,0:T(8,128)(2,1)S(1)}, u32[]{:S(2)}, u32[]{:S(2)}) collective-permute-start(bf16[2,128,128]{2,1,0:T(8,128)(2,1)S(1)} %get-tuple-element.508), channel_id=1, source_target_pairs={{0,32},{32,64},{64,96},{96,128},{128,160},{160,192},{192,224},{224... | collective-permute-start | bytes 196616 | tf_op jit(solution)/shard_map/while/body/eval_jaxpr/ppermute | solution.py:15
  373.4 6.2 %collective-permute-start.1 = (bf16[2,128,128]{2,1,0:T(8,128)(2,1)S(1)}, bf16[2,128,128]{2,1,0:T(8,128)(2,1)S(1)}, u32[]{:S(2)}, u32[]{:S(2)}) collective-permute-start(bf16[2,128,128]{2,1,0:T(8,128)(2,1)S(1)} %get-tuple-element.509), channel_id=1, source_target_pairs={{0,32},{32,64},{64,96},{96,128},{128,160},{160,192},{192,224},{224... | collective-permute-start | bytes 196616 | tf_op jit(solution)/shard_map/while/body/eval_jaxpr/ppermute | solution.py:15
  379.6 11.8 %collective-permute-start = (bf16[2,128,128]{2,1,0:T(8,128)(2,1)S(1)}, bf16[2,128,128]{2,1,0:T(8,128)(2,1)S(1)}, u32[]{:S(2)}, u32[]{:S(2)}) collective-permute-start(bf16[2,128,128]{2,1,0:T(8,128)(2,1)S(1)} %get-tuple-element.508), channel_id=1, source_target_pairs={{0,32},{32,64},{64,96},{96,128},{128,160},{160,192},{192,224},{224... | collective-permute-start | bytes 196616 | tf_op jit(solution)/shard_map/while/body/eval_jaxpr/ppermute | solution.py:15
  389.5 6.2 %collective-permute-start.1 = (bf16[2,128,128]{2,1,0:T(8,128)(2,1)S(1)}, bf16[2,128,128]{2,1,0:T(8,128)(2,1)S(1)}, u32[]{:S(2)}, u32[]{:S(2)}) collective-permute-start(bf16[2,128,128]{2,1,0:T(8,128)(2,1)S(1)} %get-tuple-element.509), channel_id=1, source_target_pairs={{0,32},{32,64},{64,96},{96,128},{128,160},{160,192},{192,224},{224... | collective-permute-start | bytes 196616 | tf_op jit(solution)/shard_map/while/body/eval_jaxpr/ppermute | solution.py:15
  395.7 10.1 %collective-permute-start = (bf16[2,128,128]{2,1,0:T(8,128)(2,1)S(1)}, bf16[2,128,128]{2,1,0:T(8,128)(2,1)S(1)}, u32[]{:S(2)}, u32[]{:S(2)}) collective-permute-start(bf16[2,128,128]{2,1,0:T(8,128)(2,1)S(1)} %get-tuple-element.508), channel_id=1, source_target_pairs={{0,32},{32,64},{64,96},{96,128},{128,160},{160,192},{192,224},{224... | collective-permute-start | bytes 196616 | tf_op jit(solution)/shard_map/while/body/eval_jaxpr/ppermute | solution.py:15
  403.8 6.2 %collective-permute-start.1 = (bf16[2,128,128]{2,1,0:T(8,128)(2,1)S(1)}, bf16[2,128,128]{2,1,0:T(8,128)(2,1)S(1)}, u32[]{:S(2)}, u32[]{:S(2)}) collective-permute-start(bf16[2,128,128]{2,1,0:T(8,128)(2,1)S(1)} %get-tuple-element.509), channel_id=1, source_target_pairs={{0,32},{32,64},{64,96},{96,128},{128,160},{160,192},{192,224},{224... | collective-permute-start | bytes 196616 | tf_op jit(solution)/shard_map/while/body/eval_jaxpr/ppermute | solution.py:15
  410.0 10.4 %collective-permute-start = (bf16[2,128,128]{2,1,0:T(8,128)(2,1)S(1)}, bf16[2,128,128]{2,1,0:T(8,128)(2,1)S(1)}, u32[]{:S(2)}, u32[]{:S(2)}) collective-permute-start(bf16[2,128,128]{2,1,0:T(8,128)(2,1)S(1)} %get-tuple-element.508), channel_id=1, source_target_pairs={{0,32},{32,64},{64,96},{96,128},{128,160},{160,192},{192,224},{224... | collective-permute-start | bytes 196616 | tf_op jit(solution)/shard_map/while/body/eval_jaxpr/ppermute | solution.py:15
  418.4 6.2 %collective-permute-start.1 = (bf16[2,128,128]{2,1,0:T(8,128)(2,1)S(1)}, bf16[2,128,128]{2,1,0:T(8,128)(2,1)S(1)}, u32[]{:S(2)}, u32[]{:S(2)}) collective-permute-start(bf16[2,128,128]{2,1,0:T(8,128)(2,1)S(1)} %get-tuple-element.509), channel_id=1, source_target_pairs={{0,32},{32,64},{64,96},{96,128},{128,160},{160,192},{192,224},{224... | collective-permute-start | bytes 196616 | tf_op jit(solution)/shard_map/while/body/eval_jaxpr/ppermute | solution.py:15
  424.6 11.5 %collective-permute-start = (bf16[2,128,128]{2,1,0:T(8,128)(2,1)S(1)}, bf16[2,128,128]{2,1,0:T(8,128)(2,1)S(1)}, u32[]{:S(2)}, u32[]{:S(2)}) collective-permute-start(bf16[2,128,128]{2,1,0:T(8,128)(2,1)S(1)} %get-tuple-element.508), channel_id=1, source_target_pairs={{0,32},{32,64},{64,96},{96,128},{128,160},{160,192},{192,224},{224... | collective-permute-start | bytes 196616 | tf_op jit(solution)/shard_map/while/body/eval_jaxpr/ppermute | solution.py:15
  433.9 6.8 %collective-permute-start.1 = (bf16[2,128,128]{2,1,0:T(8,128)(2,1)S(1)}, bf16[2,128,128]{2,1,0:T(8,128)(2,1)S(1)}, u32[]{:S(2)}, u32[]{:S(2)}) collective-permute-start(bf16[2,128,128]{2,1,0:T(8,128)(2,1)S(1)} %get-tuple-element.509), channel_id=1, source_target_pairs={{0,32},{32,64},{64,96},{96,128},{128,160},{160,192},{192,224},{224... | collective-permute-start | bytes 196616 | tf_op jit(solution)/shard_map/while/body/eval_jaxpr/ppermute | solution.py:15
  440.8 11.6 %collective-permute-start = (bf16[2,128,128]{2,1,0:T(8,128)(2,1)S(1)}, bf16[2,128,128]{2,1,0:T(8,128)(2,1)S(1)}, u32[]{:S(2)}, u32[]{:S(2)}) collective-permute-start(bf16[2,128,128]{2,1,0:T(8,128)(2,1)S(1)} %get-tuple-element.508), channel_id=1, source_target_pairs={{0,32},{32,64},{64,96},{96,128},{128,160},{160,192},{192,224},{224... | collective-permute-start | bytes 196616 | tf_op jit(solution)/shard_map/while/body/eval_jaxpr/ppermute | solution.py:15
  450.4 6.2 %collective-permute-start.1 = (bf16[2,128,128]{2,1,0:T(8,128)(2,1)S(1)}, bf16[2,128,128]{2,1,0:T(8,128)(2,1)S(1)}, u32[]{:S(2)}, u32[]{:S(2)}) collective-permute-start(bf16[2,128,128]{2,1,0:T(8,128)(2,1)S(1)} %get-tuple-element.509), channel_id=1, source_target_pairs={{0,32},{32,64},{64,96},{96,128},{128,160},{160,192},{192,224},{224... | collective-permute-start | bytes 196616 | tf_op jit(solution)/shard_map/while/body/eval_jaxpr/ppermute | solution.py:15
  456.6 11.8 %collective-permute-start = (bf16[2,128,128]{2,1,0:T(8,128)(2,1)S(1)}, bf16[2,128,128]{2,1,0:T(8,128)(2,1)S(1)}, u32[]{:S(2)}, u32[]{:S(2)}) collective-permute-start(bf16[2,128,128]{2,1,0:T(8,128)(2,1)S(1)} %get-tuple-element.508), channel_id=1, source_target_pairs={{0,32},{32,64},{64,96},{96,128},{128,160},{160,192},{192,224},{224... | collective-permute-start | bytes 196616 | tf_op jit(solution)/shard_map/while/body/eval_jaxpr/ppermute | solution.py:15
  466.0 6.2 %collective-permute-start.1 = (bf16[2,128,128]{2,1,0:T(8,128)(2,1)S(1)}, bf16[2,128,128]{2,1,0:T(8,128)(2,1)S(1)}, u32[]{:S(2)}, u32[]{:S(2)}) collective-permute-start(bf16[2,128,128]{2,1,0:T(8,128)(2,1)S(1)} %get-tuple-element.509), channel_id=1, source_target_pairs={{0,32},{32,64},{64,96},{96,128},{128,160},{160,192},{192,224},{224... | collective-permute-start | bytes 196616 | tf_op jit(solution)/shard_map/while/body/eval_jaxpr/ppermute | solution.py:15
  472.2 10.3 %collective-permute-start = (bf16[2,128,128]{2,1,0:T(8,128)(2,1)S(1)}, bf16[2,128,128]{2,1,0:T(8,128)(2,1)S(1)}, u32[]{:S(2)}, u32[]{:S(2)}) collective-permute-start(bf16[2,128,128]{2,1,0:T(8,128)(2,1)S(1)} %get-tuple-element.508), channel_id=1, source_target_pairs={{0,32},{32,64},{64,96},{96,128},{128,160},{160,192},{192,224},{224... | collective-permute-start | bytes 196616 | tf_op jit(solution)/shard_map/while/body/eval_jaxpr/ppermute | solution.py:15
  480.6 6.2 %collective-permute-start.1 = (bf16[2,128,128]{2,1,0:T(8,128)(2,1)S(1)}, bf16[2,128,128]{2,1,0:T(8,128)(2,1)S(1)}, u32[]{:S(2)}, u32[]{:S(2)}) collective-permute-start(bf16[2,128,128]{2,1,0:T(8,128)(2,1)S(1)} %get-tuple-element.509), channel_id=1, source_target_pairs={{0,32},{32,64},{64,96},{96,128},{128,160},{160,192},{192,224},{224... | collective-permute-start | bytes 196616 | tf_op jit(solution)/shard_map/while/body/eval_jaxpr/ppermute | solution.py:15
Sparse Core Ops, SparseCore 0:
  11.7 115.3 all-gather.2
  130.2 107.6 all-gather.4
